TPU v7x, 256 devices: a whole 4x4x8 slice. The times are simulated.
256 devices in a mesh: col: 32 (over x, y, core), sub: 8 (over z).
Axes of the slice: x: 4, y: 4, z: 8, core: 2. Of those that a mesh axis runs over, the one named last changes fastest.
Arguments:
- vectors: bfloat16 [1048576, 128], P(('col', 'sub')), may hold values from -6 to 6
- near_blocks: bfloat16 [4096, 4, 256, 256], P(('col', 'sub')), may hold values from -0.1875 to 0.1875
- near_index: int32 [4096, 4], P(('col', 'sub')), may hold values from 0 to 4095, as said below
- leaf_basis: bfloat16 [4096, 32, 256], P(('col', 'sub')), may hold values from -0.375 to 0.375
- leaf_transfer: float32 [4096, 32, 32], P(('col', 'sub')), may hold values from -0.25 to 0.25
- leaf_coupling: float32 [4096, 8, 32, 32], P(('col', 'sub')), may hold values from -0.375 to 0.375
- leaf_far: int32 [4096, 8], P(('col', 'sub')), may hold values from 0 to 4095, as said below
- cluster_transfer: float32 [256, 32, 32], P(('col', 'sub')), may hold values from -0.375 to 0.375
- cluster_coupling: float32 [256, 4, 32, 32], P(('col', 'sub')), may hold values from -0.5 to 0.5
- cluster_partner: int32 [256, 4], P(('col', 'sub')), may hold values from 0 to 7
- top_coupling: float32 [32, 8, 32, 32], P('col'), may hold values from -0.375 to 0.375
- top_partner: int32 [32, 8], P('col'), may hold values from 0 to 31
Outputs:
- products: bfloat16 [1048576, 128], P(('col', 'sub'))
Inputs may be any that keep to these rules, and one draw needn't show every extreme that they name: `near_index`: slot 0 of leaf i is i itself; every entry lies within 16 leaves of i; slot 1 is exactly 16 leaves away from i. `leaf_far`: every entry lies within 16 leaves of its row leaf i; slots 0 and 1 are exactly 16 leaves away from i.
All inputs are finite; a program needn't handle non-finite values.
Results may differ from a plain program's by a relative error of at most 0.0034.
Values may be sent and summed in bfloat16 or wider, within the bound.
A program may use at most 64 MiB of HBM per device.

v0:
```python
import jax
import jax.numpy as jnp
from jax import lax
from jax.sharding import PartitionSpec as P

HIGHEST = lax.Precision.HIGHEST


def with_halo(block, sides, width):
    for axis, dim in sides:
        count = lax.axis_size(axis)
        forward = [(i, i + 1) for i in range(count - 1)]
        backward = [(target, source) for source, target in forward]
        low = lax.ppermute(
            lax.slice_in_dim(block, block.shape[dim] - width, None, axis=dim), axis, forward
        )
        high = lax.ppermute(lax.slice_in_dim(block, 0, width, axis=dim), axis, backward)
        block = jnp.concatenate([low, block, high], axis=dim)
    return block


def local(
    vectors,
    near_blocks,
    near_index,
    leaf_basis,
    leaf_transfer,
    leaf_coupling,
    leaf_far,
    cluster_transfer,
    cluster_coupling,
    cluster_partner,
    top_coupling,
    top_partner,
):
    leaves_here = leaf_basis.shape[0]
    leaf_rows = leaf_basis.shape[2]
    columns = vectors.shape[1]
    window_start = lax.axis_index(("col", "sub")) * leaves_here - leaves_here
    widened = with_halo(vectors, ((("col", "sub"), 0),), leaves_here * leaf_rows)
    window_vec = widened.reshape(3 * leaves_here, leaf_rows, columns)
    own_vec = vectors.reshape(leaves_here, leaf_rows, columns)
    leaf_coefs = jnp.einsum("lrp,lpc->lrc", leaf_basis, own_vec, preferred_element_type=jnp.float32)
    window_coefs = with_halo(leaf_coefs, ((("col", "sub"), 0),), leaves_here)
    cluster_coef = jnp.einsum("lrs,lrc->sc", leaf_transfer, leaf_coefs, precision=HIGHEST)
    sub_coefs = lax.all_gather(cluster_coef[None], "sub", axis=0, tiled=True)
    cluster_field = jnp.einsum(
        "krs,ksc->rc", cluster_coupling[0], sub_coefs[cluster_partner[0]], precision=HIGHEST
    )
    upward = jnp.dot(cluster_transfer[0].T, cluster_coef, precision=HIGHEST)
    top_coef = lax.psum(upward, "sub")
    col_coefs = lax.all_gather(top_coef[None], "col", axis=0, tiled=True)
    top_field = jnp.einsum(
        "krs,ksc->rc", top_coupling[0], col_coefs[top_partner[0]], precision=HIGHEST
    )
    cluster_field = cluster_field + jnp.dot(cluster_transfer[0], top_field, precision=HIGHEST)
    far_coefs = window_coefs[leaf_far - window_start]
    leaf_field = jnp.einsum("lkrs,lksc->lrc", leaf_coupling, far_coefs, precision=HIGHEST)
    leaf_field = leaf_field + jnp.einsum(
        "lrs,sc->lrc", leaf_transfer, cluster_field, precision=HIGHEST
    )
    rounded = leaf_field.astype(jnp.bfloat16)
    picked = window_vec[near_index - window_start]
    near_part = jnp.einsum(
        "lkij,lkjc->lic", near_blocks, picked, preferred_element_type=jnp.float32
    )
    far_part = jnp.einsum("lrp,lrc->lpc", leaf_basis, rounded, preferred_element_type=jnp.float32)
    return (near_part + far_part).astype(jnp.bfloat16).reshape(leaves_here * leaf_rows, columns)


def solution(mesh):
    in_specs = (
        P(("col", "sub"), None),
        P(("col", "sub"), None, None, None),
        P(("col", "sub"), None),
        P(("col", "sub"), None, None),
        P(("col", "sub"), None, None),
        P(("col", "sub"), None, None, None),
        P(("col", "sub"), None),
        P(("col", "sub"), None, None),
        P(("col", "sub"), None, None, None),
        P(("col", "sub"), None),
        P("col", None, None, None),
        P("col", None),
    )
    out_specs = P(("col", "sub"), None)
    return jax.shard_map(local, mesh=mesh, in_specs=in_specs, out_specs=out_specs, check_vma=False)
```

profile of v0, /device:TPU:1, one launch (start us, length us, event | category | flops | bytes accessed | tf_op | source)
XLA Modules:
  0.0 154.2 jit_solution(7868082268854348627)
XLA Ops:
  0.0 0.0 copy-start
  0.0 0.0 copy-start.5
  0.0 0.0 copy-start.4
  0.0 1.7 %fusion.12 = f32[16,32,128]{2,1,0:T(8,128)S(1)} fusion(bf16[16,32,256]{2,1,0:T(8,128)(2,1)} %param.15, bf16[16,256,128]{2,1,0:T(8,128)(2,1)} %bitcast.79), kind=kOutput, calls=%fused_computation.33 | convolution fusion | flops 33554432 | bytes 1572864 | tf_op jit(solution)/shard_map/lrp,lpc->lrc/dot_general | solution.py:43
  1.7 8.9 %collective-permute-start.3 = (f32[16,32,128]{2,1,0:T(8,128)S(1)}, f32[16,32,128]{2,1,0:T(8,128)S(1)}, u32[]{:S(2)}, u32[]{:S(2)}) collective-permute-start(f32[16,32,128]{2,1,0:T(8,128)S(1)} %fusion.12), channel_id=1, source_target_pairs={{1,0},{2,1},{3,2},{4,3},{5,4},{6,5},{7,6},{8,7},{9,8},{10,9},{11,1... | collective-permute-start | bytes 786440 | tf_op jit(solution)/shard_map/ppermute | solution.py:17
  10.6 1.9 %collective-permute-start.2 = (f32[16,32,128]{2,1,0:T(8,128)S(1)}, f32[16,32,128]{2,1,0:T(8,128)}, u32[]{:S(2)}, u32[]{:S(2)}) collective-permute-start(f32[16,32,128]{2,1,0:T(8,128)S(1)} %fusion.12), channel_id=1, source_target_pairs={{0,1},{1,2},{2,3},{3,4},{4,5},{5,6},{6,7},{7,8},{8,9},{9,10},{10,1... | collective-permute-start | bytes 786440 | tf_op jit(solution)/shard_map/ppermute | solution.py:14
  12.5 4.9 %collective-permute-start.1 = (bf16[4096,128]{1,0:T(8,128)(2,1)}, bf16[4096,128]{1,0:T(8,128)(2,1)}, u32[]{:S(2)}, u32[]{:S(2)}) collective-permute-start(bf16[4096,128]{1,0:T(8,128)(2,1)} %param.12), channel_id=1, source_target_pairs={{1,0},{2,1},{3,2},{4,3},{5,4},{6,5},{7,6},{8,7},{9,8},{10,9},{11,1... | collective-permute-start | bytes 3145736 | tf_op jit(solution)/shard_map/ppermute | solution.py:17
  17.4 1.9 %collective-permute-start = (bf16[4096,128]{1,0:T(8,128)(2,1)}, bf16[4096,128]{1,0:T(8,128)(2,1)}, u32[]{:S(2)}, u32[]{:S(2)}) collective-permute-start(bf16[4096,128]{1,0:T(8,128)(2,1)} %param.12), channel_id=1, source_target_pairs={{0,1},{1,2},{2,3},{3,4},{4,5},{5,6},{6,7},{7,8},{8,9},{9,10},{10,1... | collective-permute-start | bytes 3145736 | tf_op jit(solution)/shard_map/ppermute | solution.py:14
  19.3 0.7 fusion.10
  20.0 0.7 fusion.11
  20.7 1.3 compare_select_fusion.1
  21.9 0.7 compare_select_fusion
  22.6 0.6 pad_clamp_fusion
  23.2 0.1 copy.24
  23.3 0.6 reshape.78
  23.9 1.5 fusion.13
  25.4 0.9 convolution_bitcast_fusion.3
  26.4 35.0 %psum.7 = f32[1,32,128]{2,1,0:T(8,128)S(1)} all-reduce(f32[1,32,128]{2,1,0:T(8,128)S(1)} %convolution_bitcast_fusion.3), channel_id=1, replica_groups=mesh['col'=32,'sub'=8] {'sub'}, use_global_device_ids=true, to_apply=%region_0.0 | all-reduce | flops 4096 | bytes 32768 | tf_op jit(solution)/shard_map/psum | solution.py:51
  61.4 18.5 %all-gather = f32[256,128]{1,0:T(8,128)S(1)} all-gather(f32[32,128]{1,0:T(8,128)S(1)} %bitcast.81), channel_id=2, replica_groups=mesh['col'=32,'sub'=8] {'sub'}, dimensions={0}, use_global_device_ids=true | all-gather | bytes 147456 | tf_op jit(solution)/shard_map/all_gather | solution.py:46
  79.9 36.2 %all_gather.7 = f32[32,32,128]{2,1,0:T(8,128)S(1)} all-gather(f32[1,32,128]{2,1,0:T(8,128)S(1)} %psum.7), channel_id=1, replica_groups=mesh['col'=32,'sub'=8] {'col'}, dimensions={0}, use_global_device_ids=true | all-gather | bytes 540672 | tf_op jit(solution)/shard_map/all_gather | solution.py:52
  116.1 0.6 gather_fusion.2
  116.6 0.0 copy-done.5
  116.6 0.2 convolution_bitcast_fusion.4
  116.9 0.7 gather_fusion.3
  117.6 0.0 copy-done.4
  117.6 0.3 convolution_bitcast_fusion.2
  117.9 0.6 pad_clamp_fusion.2
  118.5 0.7 copy.22
  119.3 0.1 reshape.70
  119.4 0.9 fusion.4
  120.2 0.0 collective-permute-done.3
  120.3 0.0 collective-permute-done.2
  120.3 1.0 pad_maximum_fusion.1
  121.3 2.1 %gather_fusion.1 = f32[128,32,128]{2,1,0:T(8,128)} fusion(f32[48,32,128]{2,1,0:T(8,128)S(1)} %pad_maximum_fusion.1, s32[1024]{0:T(1024)S(1)} %pad_clamp_fusion.2), kind=kCustom, calls=%fused_computation.1 | custom fusion | bytes 4194816 | tf_op jit(solution)/shard_map/gather | solution.py:57
  123.4 0.0 copy-start.3
  123.4 0.0 copy-done
  123.4 4.4 %convolution_bitcast_fusion.1 = f32[16,32,128]{2,1,0:T(8,128)S(1)} fusion(f32[16,8,32,128]{3,2,1,0:T(8,128)} %bitcast.78, f32[16,8,32,32]{3,2,1,0:T(8,128)S(1)} %copy-done), kind=kOutput, calls=%fused_computation.10 | convolution fusion | flops 201326592 | bytes 2883584 | tf_op jit(solution)/shard_map/lkrs,lksc->lrc/dot_general | solution.py:58
  127.9 0.0 copy-done.3
  127.9 0.4 fusion.3
  128.2 0.0 copy-done.2
  128.2 1.9 %fusion.14 = f32[16,128,256]{2,1,0:T(8,128)} fusion(bf16[16,32,128]{2,1,0:T(8,128)(2,1)S(1)} %fusion.3, bf16[16,32,256]{2,1,0:T(8,128)(2,1)S(1)} %copy-done.2), kind=kOutput, calls=%fused_computation.35 | convolution fusion | flops 33554432 | bytes 2490368 | tf_op jit(solution)/shard_map/lrp,lrc->lpc/dot_general | solution.py:67
  130.1 0.0 collective-permute-done.1
  130.1 0.0 collective-permute-done
  130.1 0.0 copy-done.1
  130.1 9.8 %pad_maximum_fusion = bf16[12288,128]{1,0:T(8,128)(2,1)} fusion(bf16[4096,128]{1,0:T(8,128)(2,1)} %collective-permute-done.1, bf16[4096,128]{1,0:T(8,128)(2,1)S(1)} %copy-done.1, bf16[4096,128]{1,0:T(8,128)(2,1)} %collective-permute-done), kind=kLoop, calls=%fused_computation.4 | loop fusion | flops 9437184 | bytes 6291456 | tf_op jit(solution)/shard_map/concatenate | solution.py:18
  139.9 4.9 %gather_fusion = bf16[64,256,128]{2,1,0:T(8,128)(2,1)} fusion(bf16[48,256,128]{2,1,0:T(8,128)(2,1)} %bitcast.76, s32[1024]{0:T(1024)S(1)} %pad_clamp_fusion.3), kind=kCustom, calls=%fused_computation | custom fusion | bytes 8388864 | tf_op jit(solution)/shard_map/gather | solution.py:63
  144.8 8.1 %fusion.1 = bf16[16,256,128]{1,2,0:T(8,128)(2,1)S(1)} fusion(f32[16,128,256]{2,1,0:T(8,128)} %fusion.14, bf16[16,4,256,128]{3,2,1,0:T(8,128)(2,1)} %bitcast.77, bf16[16,4,256,256]{3,2,1,0:T(8,128)(2,1)} %param.13), kind=kOutput, calls=%fused_computation.7 | convolution fusion | flops 1074790400 | bytes 15728640 | tf_op jit(solution)/shard_map/lkij,lkjc->lic/dot_general | solution.py:64
  152.9 1.3 copy.26
  (4 shorter events, 0.0 us)
Async XLA Ops:
  0.0 123.4 %copy-start = (f32[16,8,32,32]{3,2,1,0:T(8,128)S(1)}, f32[16,8,32,32]{3,2,1,0:T(8,128)}, u32[]{:S(2)}) copy-start(f32[16,8,32,32]{3,2,1,0:T(8,128)} %param.17) | copy-start | bytes 1572868
  0.0 116.6 %copy-start.5 = (f32[1,4,32,32]{3,2,1,0:T(8,128)S(1)}, f32[1,4,32,32]{3,2,1,0:T(8,128)}, u32[]{:S(2)}) copy-start(f32[1,4,32,32]{3,2,1,0:T(8,128)} %param.20) | copy-start | bytes 49156
  0.0 117.6 %copy-start.4 = (f32[1,8,32,32]{3,2,1,0:T(8,128)S(1)}, f32[1,8,32,32]{3,2,1,0:T(8,128)}, u32[]{:S(2)}) copy-start(f32[1,8,32,32]{3,2,1,0:T(8,128)} %param.22) | copy-start | bytes 98308
  1.7 118.5 %collective-permute-start.3 = (f32[16,32,128]{2,1,0:T(8,128)S(1)}, f32[16,32,128]{2,1,0:T(8,128)S(1)}, u32[]{:S(2)}, u32[]{:S(2)}) collective-permute-start(f32[16,32,128]{2,1,0:T(8,128)S(1)} %fusion.12), channel_id=1, source_target_pairs={{1,0},{2,1},{3,2},{4,3},{5,4},{6,5},{7,6},{8,7},{9,8},{10,9},{11,1... | collective-permute-start | bytes 786440 | tf_op jit(solution)/shard_map/ppermute | solution.py:17
  10.6 109.6 %collective-permute-start.2 = (f32[16,32,128]{2,1,0:T(8,128)S(1)}, f32[16,32,128]{2,1,0:T(8,128)}, u32[]{:S(2)}, u32[]{:S(2)}) collective-permute-start(f32[16,32,128]{2,1,0:T(8,128)S(1)} %fusion.12), channel_id=1, source_target_pairs={{0,1},{1,2},{2,3},{3,4},{4,5},{5,6},{6,7},{7,8},{8,9},{9,10},{10,1... | collective-permute-start | bytes 786440 | tf_op jit(solution)/shard_map/ppermute | solution.py:14
  12.5 117.6 %collective-permute-start.1 = (bf16[4096,128]{1,0:T(8,128)(2,1)}, bf16[4096,128]{1,0:T(8,128)(2,1)}, u32[]{:S(2)}, u32[]{:S(2)}) collective-permute-start(bf16[4096,128]{1,0:T(8,128)(2,1)} %param.12), channel_id=1, source_target_pairs={{1,0},{2,1},{3,2},{4,3},{5,4},{6,5},{7,6},{8,7},{9,8},{10,9},{11,1... | collective-permute-start | bytes 3145736 | tf_op jit(solution)/shard_map/ppermute | solution.py:17
  17.4 112.7 %collective-permute-start = (bf16[4096,128]{1,0:T(8,128)(2,1)}, bf16[4096,128]{1,0:T(8,128)(2,1)}, u32[]{:S(2)}, u32[]{:S(2)}) collective-permute-start(bf16[4096,128]{1,0:T(8,128)(2,1)} %param.12), channel_id=1, source_target_pairs={{0,1},{1,2},{2,3},{3,4},{4,5},{5,6},{6,7},{7,8},{8,9},{9,10},{10,1... | collective-permute-start | bytes 3145736 | tf_op jit(solution)/shard_map/ppermute | solution.py:14
  123.4 4.4 %copy-start.3 = (f32[16,32,32]{2,1,0:T(8,128)S(1)}, f32[16,32,32]{2,1,0:T(8,128)}, u32[]{:S(2)}) copy-start(f32[16,32,32]{2,1,0:T(8,128)} %param.16) | copy-start | bytes 196612
  123.4 4.8 %copy-start.2 = (bf16[16,32,256]{2,1,0:T(8,128)(2,1)S(1)}, bf16[16,32,256]{2,1,0:T(8,128)(2,1)}, u32[]{:S(2)}) copy-start(bf16[16,32,256]{2,1,0:T(8,128)(2,1)} %param.15) | copy-start | bytes 786436
  123.4 6.7 %copy-start.1 = (bf16[4096,128]{1,0:T(8,128)(2,1)S(1)}, bf16[4096,128]{1,0:T(8,128)(2,1)}, u32[]{:S(2)}) copy-start(bf16[4096,128]{1,0:T(8,128)(2,1)} %param.12) | copy-start | bytes 3145732
where the time goes:
time: 155 us; the launch traced here: 154 us
  blocking collectives  89.7 us (58%)
  matrix products  20.3 us (13%)
  starting transfers between devices  17.6 us (11%)
  other arithmetic  15.3 us (10%)
  local copies, waits for them, and re-layouts  11.1 us (7%)
    all_gather x1, blocking collectives, local(): col_coefs = lax.all_gather(top_coef[None], 'col', axis=0, tiled=True)  36.2 us
    psum x1, blocking collectives, local(): top_coef = lax.psum(upward, 'sub')  35 us
    all_gather x1, blocking collectives, local(): sub_coefs = lax.all_gather(cluster_coef[None], 'sub', axis=0, tiled=True)  18.5 us
    ppermute x2, starting transfers between devices, with_halo(): lax.ppermute(lax.slice_in_dim(block, 0, width, axis=dim), axis, backward)  13.7 us
    concatenate x2, other arithmetic, with_halo(): block = jnp.concatenate([low, block, high], axis=dim)  10.8 us
    dot_general x1, matrix products, local(): jnp.einsum('lkij,lkjc->lic', near_blocks, picked, preferred_element_type=...  8.06 us
    gather x1, local copies, waits for them, and re-layouts, local(): picked = window_vec[near_index - window_start]  4.91 us
    dot_general x1, matrix products, local(): jnp.einsum('lkrs,lksc->lrc', leaf_coupling, far_coefs, precision=HIGHEST)  4.43 us
  transfers between devices with their start and end apart: 4, of which 0 were waited for; matrix products, arithmetic and copies ran while one was open for 14% of the time, Pallas kernels for 0%

commit v1 on v0

--- a/solution.py
+++ b/solution.py
@@ -2,6 +2,7 @@
 import jax.numpy as jnp
 from jax import lax
 from jax.sharding import PartitionSpec as P
+from jax.lax import ppermute, psum
 
 HIGHEST = lax.Precision.HIGHEST
 
@@ -48,7 +49,10 @@
         "krs,ksc->rc", cluster_coupling[0], sub_coefs[cluster_partner[0]], precision=HIGHEST
     )
     upward = jnp.dot(cluster_transfer[0].T, cluster_coef, precision=HIGHEST)
-    top_coef = lax.psum(upward, "sub")
+    n_shards = psum(1, axis_name="sub")
+    top_coef = upward
+    for t in [[(p, p ^ it) for p in range(n_shards)] for it in (1, 2, 4, 8, 16) if it < n_shards]:
+        top_coef = top_coef + ppermute(top_coef, perm=t, axis_name="sub")
     col_coefs = lax.all_gather(top_coef[None], "col", axis=0, tiled=True)
     top_field = jnp.einsum(
         "krs,ksc->rc", top_coupling[0], col_coefs[top_partner[0]], precision=HIGHEST

time: 155 us -> 142 us (0.916)
  blocking collectives: 89.7 us -> 67.7 us
  waiting for transfers between devices: 0.01 us -> 8.63 us
  matrix products: 20.3 us -> 22.3 us
  other arithmetic: 15.3 us -> 13.5 us
    psum x1 -> x0, blocking collectives: 35 us -> none  [local(): top_coef = lax.psum(upward, 'sub')]
    all_gather x1, blocking collectives: 18.5 us -> 35.9 us  [local(): sub_coefs = lax.all_gather(cluster_coef[None], 'sub', axis=0, tiled=True)]
    ppermute x0 -> x3, waiting for transfers between devices: none -> 8.62 us  [local(): top_coef = top_coef + ppermute(top_coef, perm=t, axis_name='sub')]
    all_gather x1, blocking collectives: 36.2 us -> 31.8 us  [local(): col_coefs = lax.all_gather(top_coef[None], 'col', axis=0, tiled=True)]
  transfers between devices with their start and end apart: 4 -> 7, of which waited for: 0 -> 2; matrix products, arithmetic and copies ran while one was open for 14% -> 14% of each run, Pallas kernels for 0% -> 0%
where the time goes in v1:
time: 142 us; the launch traced here: 141 us
  blocking collectives  67.7 us (48%)
  matrix products  22.3 us (16%)
  starting transfers between devices  18.9 us (13%)
  other arithmetic  13.5 us (10%)
  local copies, waits for them, and re-layouts  9.81 us (7%)
  waiting for transfers between devices  8.63 us (6%)
    all_gather x1, blocking collectives, local(): sub_coefs = lax.all_gather(cluster_coef[None], 'sub', axis=0, tiled=True)  35.9 us
    all_gather x1, blocking collectives, local(): col_coefs = lax.all_gather(top_coef[None], 'col', axis=0, tiled=True)  31.8 us
    ppermute x2, starting transfers between devices, with_halo(): lax.ppermute(lax.slice_in_dim(block, 0, width, axis=dim), axis, backward)  13.7 us
    concatenate x2, other arithmetic, with_halo(): block = jnp.concatenate([low, block, high], axis=dim)  10.8 us
    ppermute x3, waiting for transfers between devices, local(): top_coef = top_coef + ppermute(top_coef, perm=t, axis_name='sub')  8.62 us
    dot_general x1, matrix products, local(): jnp.einsum('lkij,lkjc->lic', near_blocks, picked, preferred_element_type=...  8.07 us
    gather x1, local copies, waits for them, and re-layouts, local(): picked = window_vec[near_index - window_start]  4.93 us
    dot_general x1, matrix products, local(): jnp.einsum('lkrs,lksc->lrc', leaf_coupling, far_coefs, precision=HIGHEST)  4.43 us
  transfers between devices with their start and end apart: 7, of which 2 were waited for; matrix products, arithmetic and copies ran while one was open for 14% of the time, Pallas kernels for 0%

profile of v1, /device:TPU:1, one launch (start us, length us, event | category | flops | bytes accessed | tf_op | source)
XLA Modules:
  0.0 141.1 jit_solution(11692562266316405104)
XLA Ops:
  0.0 0.0 copy-start
  0.0 0.0 copy-start.4
  0.0 1.7 %fusion.12 = f32[16,32,128]{2,1,0:T(8,128)S(1)} fusion(bf16[16,32,256]{2,1,0:T(8,128)(2,1)} %param.15, bf16[16,256,128]{2,1,0:T(8,128)(2,1)} %bitcast.78), kind=kOutput, calls=%fused_computation.33 | convolution fusion | flops 33554432 | bytes 1572864 | tf_op jit(solution)/shard_map/lrp,lpc->lrc/dot_general | solution.py:44
  1.7 8.9 %collective-permute-start.3 = (f32[16,32,128]{2,1,0:T(8,128)S(1)}, f32[16,32,128]{2,1,0:T(8,128)S(1)}, u32[]{:S(2)}, u32[]{:S(2)}) collective-permute-start(f32[16,32,128]{2,1,0:T(8,128)S(1)} %fusion.12), channel_id=1, source_target_pairs={{1,0},{2,1},{3,2},{4,3},{5,4},{6,5},{7,6},{8,7},{9,8},{10,9},{11,1... | collective-permute-start | bytes 786440 | tf_op jit(solution)/shard_map/ppermute | solution.py:18
  10.6 1.9 %collective-permute-start.2 = (f32[16,32,128]{2,1,0:T(8,128)S(1)}, f32[16,32,128]{2,1,0:T(8,128)}, u32[]{:S(2)}, u32[]{:S(2)}) collective-permute-start(f32[16,32,128]{2,1,0:T(8,128)S(1)} %fusion.12), channel_id=1, source_target_pairs={{0,1},{1,2},{2,3},{3,4},{4,5},{5,6},{6,7},{7,8},{8,9},{9,10},{10,1... | collective-permute-start | bytes 786440 | tf_op jit(solution)/shard_map/ppermute | solution.py:15
  12.5 4.9 %collective-permute-start.1 = (bf16[4096,128]{1,0:T(8,128)(2,1)}, bf16[4096,128]{1,0:T(8,128)(2,1)}, u32[]{:S(2)}, u32[]{:S(2)}) collective-permute-start(bf16[4096,128]{1,0:T(8,128)(2,1)} %param.12), channel_id=1, source_target_pairs={{1,0},{2,1},{3,2},{4,3},{5,4},{6,5},{7,6},{8,7},{9,8},{10,9},{11,1... | collective-permute-start | bytes 3145736 | tf_op jit(solution)/shard_map/ppermute | solution.py:18
  17.4 1.9 %collective-permute-start = (bf16[4096,128]{1,0:T(8,128)(2,1)}, bf16[4096,128]{1,0:T(8,128)(2,1)}, u32[]{:S(2)}, u32[]{:S(2)}) collective-permute-start(bf16[4096,128]{1,0:T(8,128)(2,1)} %param.12), channel_id=1, source_target_pairs={{0,1},{1,2},{2,3},{3,4},{4,5},{5,6},{6,7},{7,8},{8,9},{9,10},{10,1... | collective-permute-start | bytes 3145736 | tf_op jit(solution)/shard_map/ppermute | solution.py:15
  19.3 1.5 %fusion.13 = f32[128,32,1]{0,1,2:T(8,128)S(1)} fusion(f32[16,32,128]{2,1,0:T(8,128)S(1)} %fusion.12, f32[16,32,32]{2,1,0:T(8,128)} %param.16), kind=kOutput, calls=%fused_computation.34 | convolution fusion | flops 25165824 | bytes 344064 | tf_op jit(solution)/shard_map/lrs,lrc->sc/dot_general | solution.py:46
  20.9 0.9 convolution_bitcast_fusion.4
  21.8 0.1 collective-permute-start.4
  21.9 0.7 fusion.10
  22.6 0.7 fusion.11
  23.2 0.7 compare_select_fusion.1
  23.9 0.7 compare_select_fusion
  24.6 35.9 %all-gather = f32[256,128]{1,0:T(8,128)S(1)} all-gather(f32[32,128]{1,0:T(8,128)S(1)} %bitcast.81), channel_id=2, replica_groups=mesh['col'=32,'sub'=8] {'sub'}, dimensions={0}, use_global_device_ids=true | all-gather | bytes 147456 | tf_op jit(solution)/shard_map/all_gather | solution.py:47
  60.5 0.6 gather_fusion.2
  61.1 1.4 %convolution_bitcast_fusion.3 = f32[128,32]{1,0:T(8,128)S(1)} fusion(f32[4,32,128]{2,1,0:T(8,128)S(1)} %gather_fusion.2, f32[1,4,32,32]{3,2,1,0:T(8,128)} %param.20), kind=kOutput, calls=%fused_computation.15 | convolution fusion | flops 6291456 | bytes 98304 | tf_op jit(solution)/shard_map/krs,ksc->rc/dot_general | solution.py:48
  62.5 0.1 copy.19
  62.6 0.1 reshape.78
  62.7 0.0 collective-permute-done.4
  62.7 0.1 collective-permute-start.5
  62.8 0.1 copy.17
  62.9 0.1 reshape.70
  63.0 3.3 %collective-permute-done.5 = f32[32,128]{1,0:T(8,128)S(1)} collective-permute-done((f32[32,128]{1,0:T(8,128)S(1)}, f32[32,128]{1,0:T(8,128)S(1)}, u32[]{:S(2)}, u32[]{:S(2)}) %collective-permute-start.5) | collective-permute-done | bytes 16416 | tf_op jit(solution)/shard_map/ppermute | solution.py:55
  66.3 1.2 collective-permute-start.6
  67.5 5.3 %collective-permute-done.6 = f32[32,128]{1,0:T(8,128)S(1)} collective-permute-done((f32[32,128]{1,0:T(8,128)S(1)}, f32[32,128]{1,0:T(8,128)S(1)}, u32[]{:S(2)}, u32[]{:S(2)}) %collective-permute-start.6) | collective-permute-done | bytes 16416 | tf_op jit(solution)/shard_map/ppermute | solution.py:55
  72.8 31.8 %all-gather.1 = f32[1024,128]{1,0:T(8,128)S(1)} all-gather(f32[32,128]{1,0:T(8,128)S(1)} %add.64), channel_id=3, replica_groups=mesh['col'=32,'sub'=8] {'col'}, dimensions={0}, use_global_device_ids=true | all-gather | bytes 540672 | tf_op jit(solution)/shard_map/all_gather | solution.py:56
  104.6 0.6 gather_fusion.3
  105.2 0.0 copy-done.4
  105.2 1.0 convolution_bitcast_fusion.2
  106.2 0.9 fusion.4
  107.1 0.0 collective-permute-done.3
  107.1 0.0 collective-permute-done.2
  107.1 1.0 pad_maximum_fusion.1
  108.1 2.1 %gather_fusion.1 = f32[128,32,128]{2,1,0:T(8,128)} fusion(f32[48,32,128]{2,1,0:T(8,128)S(1)} %pad_maximum_fusion.1, s32[1024]{0:T(1024)S(1)} %pad_clamp_fusion.2), kind=kCustom, calls=%fused_computation.1 | custom fusion | bytes 4194816 | tf_op jit(solution)/shard_map/gather | solution.py:61
  110.2 0.0 copy-done
  110.3 4.4 %convolution_bitcast_fusion.1 = f32[16,32,128]{2,1,0:T(8,128)S(1)} fusion(f32[16,8,32,128]{3,2,1,0:T(8,128)} %bitcast.77, f32[16,8,32,32]{3,2,1,0:T(8,128)S(1)} %copy-done), kind=kOutput, calls=%fused_computation.10 | convolution fusion | flops 201326592 | bytes 2883584 | tf_op jit(solution)/shard_map/lkrs,lksc->lrc/dot_general | solution.py:62
  114.7 0.0 copy-done.3
  114.7 0.4 fusion.3
  115.1 0.0 copy-done.2
  115.1 1.9 %fusion.14 = f32[16,128,256]{2,1,0:T(8,128)} fusion(bf16[16,32,128]{2,1,0:T(8,128)(2,1)S(1)} %fusion.3, bf16[16,32,256]{2,1,0:T(8,128)(2,1)S(1)} %copy-done.2), kind=kOutput, calls=%fused_computation.35 | convolution fusion | flops 33554432 | bytes 2490368 | tf_op jit(solution)/shard_map/lrp,lrc->lpc/dot_general | solution.py:71
  117.0 0.0 collective-permute-done.1
  117.0 0.0 collective-permute-done
  117.0 0.0 copy-done.1
  117.0 9.8 %pad_maximum_fusion = bf16[12288,128]{1,0:T(8,128)(2,1)} fusion(bf16[4096,128]{1,0:T(8,128)(2,1)} %collective-permute-done.1, bf16[4096,128]{1,0:T(8,128)(2,1)S(1)} %copy-done.1, bf16[4096,128]{1,0:T(8,128)(2,1)} %collective-permute-done), kind=kLoop, calls=%fused_computation.4 | loop fusion | flops 9437184 | bytes 6291456 | tf_op jit(solution)/shard_map/concatenate | solution.py:19
  126.8 4.9 %gather_fusion = bf16[64,256,128]{2,1,0:T(8,128)(2,1)} fusion(bf16[48,256,128]{2,1,0:T(8,128)(2,1)} %bitcast.75, s32[1024]{0:T(1024)S(1)} %pad_clamp_fusion.3), kind=kCustom, calls=%fused_computation | custom fusion | bytes 8388864 | tf_op jit(solution)/shard_map/gather | solution.py:67
  131.7 8.1 %fusion.1 = bf16[16,256,128]{1,2,0:T(8,128)(2,1)S(1)} fusion(f32[16,128,256]{2,1,0:T(8,128)} %fusion.14, bf16[16,4,256,128]{3,2,1,0:T(8,128)(2,1)} %bitcast.76, bf16[16,4,256,256]{3,2,1,0:T(8,128)(2,1)} %param.13), kind=kOutput, calls=%fused_computation.7 | convolution fusion | flops 1074790400 | bytes 15728640 | tf_op jit(solution)/shard_map/lkij,lkjc->lic/dot_general | solution.py:68
  139.8 1.3 copy.21
  (10 shorter events, 0.0 us)
Async XLA Ops:
  0.0 110.2 %copy-start = (f32[16,8,32,32]{3,2,1,0:T(8,128)S(1)}, f32[16,8,32,32]{3,2,1,0:T(8,128)}, u32[]{:S(2)}) copy-start(f32[16,8,32,32]{3,2,1,0:T(8,128)} %param.17) | copy-start | bytes 1572868
  0.0 105.2 %copy-start.4 = (f32[1,8,32,32]{3,2,1,0:T(8,128)S(1)}, f32[1,8,32,32]{3,2,1,0:T(8,128)}, u32[]{:S(2)}) copy-start(f32[1,8,32,32]{3,2,1,0:T(8,128)} %param.22) | copy-start | bytes 98308
  1.7 105.4 %collective-permute-start.3 = (f32[16,32,128]{2,1,0:T(8,128)S(1)}, f32[16,32,128]{2,1,0:T(8,128)S(1)}, u32[]{:S(2)}, u32[]{:S(2)}) collective-permute-start(f32[16,32,128]{2,1,0:T(8,128)S(1)} %fusion.12), channel_id=1, source_target_pairs={{1,0},{2,1},{3,2},{4,3},{5,4},{6,5},{7,6},{8,7},{9,8},{10,9},{11,1... | collective-permute-start | bytes 786440 | tf_op jit(solution)/shard_map/ppermute | solution.py:18
  10.6 96.5 %collective-permute-start.2 = (f32[16,32,128]{2,1,0:T(8,128)S(1)}, f32[16,32,128]{2,1,0:T(8,128)}, u32[]{:S(2)}, u32[]{:S(2)}) collective-permute-start(f32[16,32,128]{2,1,0:T(8,128)S(1)} %fusion.12), channel_id=1, source_target_pairs={{0,1},{1,2},{2,3},{3,4},{4,5},{5,6},{6,7},{7,8},{8,9},{9,10},{10,1... | collective-permute-start | bytes 786440 | tf_op jit(solution)/shard_map/ppermute | solution.py:15
  12.5 104.4 %collective-permute-start.1 = (bf16[4096,128]{1,0:T(8,128)(2,1)}, bf16[4096,128]{1,0:T(8,128)(2,1)}, u32[]{:S(2)}, u32[]{:S(2)}) collective-permute-start(bf16[4096,128]{1,0:T(8,128)(2,1)} %param.12), channel_id=1, source_target_pairs={{1,0},{2,1},{3,2},{4,3},{5,4},{6,5},{7,6},{8,7},{9,8},{10,9},{11,1... | collective-permute-start | bytes 3145736 | tf_op jit(solution)/shard_map/ppermute | solution.py:18
  17.4 99.6 %collective-permute-start = (bf16[4096,128]{1,0:T(8,128)(2,1)}, bf16[4096,128]{1,0:T(8,128)(2,1)}, u32[]{:S(2)}, u32[]{:S(2)}) collective-permute-start(bf16[4096,128]{1,0:T(8,128)(2,1)} %param.12), channel_id=1, source_target_pairs={{0,1},{1,2},{2,3},{3,4},{4,5},{5,6},{6,7},{7,8},{8,9},{9,10},{10,1... | collective-permute-start | bytes 3145736 | tf_op jit(solution)/shard_map/ppermute | solution.py:15
  21.8 40.9 %collective-permute-start.4 = (f32[32,128]{1,0:T(8,128)S(1)}, f32[32,128]{1,0:T(8,128)S(1)}, u32[]{:S(2)}, u32[]{:S(2)}) collective-permute-start(f32[32,128]{1,0:T(8,128)S(1)} %convolution_bitcast_fusion.4), channel_id=1, source_target_pairs={{0,1},{1,0},{2,3},{3,2},{4,5},{5,4},{6,7},{7,6},{8,9},{9,8},{10,11... | collective-permute-start | bytes 49160 | tf_op jit(solution)/shard_map/ppermute | solution.py:55
  62.7 3.6 %collective-permute-start.5 = (f32[32,128]{1,0:T(8,128)S(1)}, f32[32,128]{1,0:T(8,128)S(1)}, u32[]{:S(2)}, u32[]{:S(2)}) collective-permute-start(f32[32,128]{1,0:T(8,128)S(1)} %add.62), channel_id=1, source_target_pairs={{0,2},{1,3},{2,0},{3,1},{4,6},{5,7},{6,4},{7,5},{8,10},{9,11},{10,... | collective-permute-start | bytes 49160 | tf_op jit(solution)/shard_map/ppermute | solution.py:55
  66.3 6.5 %collective-permute-start.6 = (f32[32,128]{1,0:T(8,128)S(1)}, f32[32,128]{1,0:T(8,128)S(1)}, u32[]{:S(2)}, u32[]{:S(2)}) collective-permute-start(f32[32,128]{1,0:T(8,128)S(1)} %add.63), channel_id=1, source_target_pairs={{0,4},{1,5},{2,6},{3,7},{4,0},{5,1},{6,2},{7,3},{8,12},{9,13},{10,... | collective-permute-start | bytes 49160 | tf_op jit(solution)/shard_map/ppermute | solution.py:55
  110.2 4.4 %copy-start.3 = (f32[16,32,32]{2,1,0:T(8,128)S(1)}, f32[16,32,32]{2,1,0:T(8,128)}, u32[]{:S(2)}) copy-start(f32[16,32,32]{2,1,0:T(8,128)} %param.16) | copy-start | bytes 196612
  110.2 4.8 %copy-start.2 = (bf16[16,32,256]{2,1,0:T(8,128)(2,1)S(1)}, bf16[16,32,256]{2,1,0:T(8,128)(2,1)}, u32[]{:S(2)}) copy-start(bf16[16,32,256]{2,1,0:T(8,128)(2,1)} %param.15) | copy-start | bytes 786436
  110.2 6.7 %copy-start.1 = (bf16[4096,128]{1,0:T(8,128)(2,1)S(1)}, bf16[4096,128]{1,0:T(8,128)(2,1)}, u32[]{:S(2)}) copy-start(bf16[4096,128]{1,0:T(8,128)(2,1)} %param.12) | copy-start | bytes 3145732
